TPU v7x, 32 devices: a whole 2x2x4 slice. The times are simulated.
32 devices in a mesh: rows: 8 (over z, y), cols: 4 (over x, core).
Axes of the slice: x: 2, y: 2, z: 4, core: 2. Of those that a mesh axis runs over, the one named last changes fastest.
Arguments:
- basis_cols: bfloat16 [32768, 1024], P('rows', 'cols'), may hold values from -6 to 6, as said below
- snapshots: bfloat16 [256, 32768], P(None, 'rows'), may hold values from -600 to 600
Outputs:
- coefficients: float32 [1024, 256], P('cols')
- factor: float32 [256, 256], replicated
- directions: bfloat16 [256, 32768], P(None, ('rows', 'cols'))
Inputs may be any that keep to these rules, and one draw needn't show every extreme that they name: `basis_cols`: normal entries.
All inputs are finite; a program needn't handle non-finite values.
Results may differ from a plain program's by a relative error of at most 0.0056.
Values may be sent and summed in bfloat16 or wider, within the bound.
No kernel may reach another device: no remote copies, remote signals or barrier semaphores. Data moves between devices by JAX's collectives and lax.ppermute only.
A program may use at most 64 MiB of HBM per device.

v0:
```python
import math
import jax
import jax.numpy as jnp
from jax import lax
from jax.sharding import PartitionSpec as P

RANK = 1024


def shards(basis_cols, snapshots):
    col_count = lax.axis_size("cols")
    column_index = lax.axis_index("cols")
    total_points = snapshots.shape[1] * lax.axis_size("rows")
    part_rows = snapshots.shape[1] // col_count
    own_snaps = lax.dynamic_slice_in_dim(snapshots, column_index * part_rows, part_rows, 1)
    coeff_scale = math.sqrt(RANK) / total_points
    partial_value = lax.dot_general(
        basis_cols, snapshots, (((0,), (1,)), ((), ())), preferred_element_type=jnp.float32
    )
    coefficients = lax.psum(partial_value, "rows") * coeff_scale
    coeff_low = coefficients.astype(jnp.bfloat16)
    recon_part = lax.dot_general(
        coeff_low, basis_cols, (((0,), (1,)), ((), ())), preferred_element_type=jnp.float32
    )
    recon = lax.psum_scatter(recon_part, "cols", scatter_dimension=1, tiled=True) / math.sqrt(RANK)
    residual = own_snaps.astype(jnp.float32) - recon
    partial_gram = jnp.dot(residual, residual.T, precision=lax.Precision.HIGHEST) / total_points
    gram = lax.psum(partial_gram, ("rows", "cols"))
    factor = jnp.linalg.cholesky(gram)
    directions = lax.linalg.triangular_solve(factor, residual, left_side=True, lower=True).astype(
        jnp.bfloat16
    )
    return (coefficients, factor, directions)


def solution(mesh):
    placed = (P("rows", "cols"), P(None, "rows"))
    return jax.shard_map(
        shards,
        mesh=mesh,
        in_specs=placed,
        out_specs=(P("cols", None), P(), P(None, ("rows", "cols"))),
        check_vma=False,
    )
```

profile of v0, /device:TPU:0, one launch (start us, length us, event | category | flops | bytes accessed | tf_op | source)
XLA Modules:
  0.0 342.6 jit_solution(12605223507592802516)
XLA Ops:
  7.2 0.0 copy-start
  7.2 0.0 all-reduce.4.cloned.1.call-start
  7.2 1.5 copy-done
  8.8 3.0 fusion.12
  11.8 0.0 all-reduce.4.cloned.1.call-update
  11.8 0.0 reduce-scatter.2.cloned.1.call-start
  11.9 73.8 %all-reduce.4.cloned.1.call-done = f32[256,256]{1,0:T(8,128)} async-done(((f32[256,256]{1,0:T(8,128)}), f32[256,256]{1,0:T(8,128)}) %all-reduce.4.cloned.1.call-update) | async-done | bytes 262160 | tf_op jit(solution)/shard_map/psum | solution.py:20
  85.7 1.0 broadcast_multiply_fusion
  86.7 0.0 copy-start.1
  86.7 2.7 fusion.4
  89.4 0.0 copy-done.1
  89.4 0.0 reduce-scatter.2.cloned.1.call-update
  89.4 0.0 all-reduce.6.cloned.1.call-start
  89.5 43.7 %reduce-scatter.2.cloned.1.call-done = f32[256,1024]{1,0:T(8,128)} async-done(((f32[256,4096]{1,0:T(8,128)}), f32[256,1024]{1,0:T(8,128)}) %reduce-scatter.2.cloned.1.call-update) | async-done | bytes 1048592 | tf_op jit(solution)/shard_map/reduce_scatter | solution.py:25
  133.2 1.5 multiply_subtract_fusion
  134.8 1.7 convolution_multiply_fusion
  136.5 0.0 all-reduce.6.cloned.1.call-update
  136.5 129.4 %all-reduce.6.cloned.1.call-done = f32[256,256]{0,1:T(8,128)} async-done(((f32[256,256]{0,1:T(8,128)}), f32[256,256]{0,1:T(8,128)}) %all-reduce.6.cloned.1.call-update) | async-done | bytes 262160 | tf_op jit(solution)/shard_map/psum | solution.py:28
  265.9 1.1 copy.6
  267.0 1.0 fusion.2
  268.0 0.0 copy-start.3
  268.0 0.7 copy-done.3
  268.7 11.7 %cholesky.50 = f32[128,128]{1,0:T(8,128)S(1)} custom-call(f32[128,128]{1,0:T(8,128)S(1)} %cholesky.118), custom_call_target="Cholesky" | custom-call | tf_op jit(solution)/shard_map/jit(cholesky)/cholesky | solution.py:29
  280.5 9.8 %custom-call.14 = f32[1,128,128]{1,2,0:T(8,128)S(1)} custom-call(f32[1,128,128]{2,1,0:T(8,128)S(1)} %get-tuple-element.26), custom_call_target="InvertDiagBlocksLowerTriangular" | custom-call | tf_op jit(solution)/shard_map/jit(cholesky)/cholesky | solution.py:29
  290.3 1.0 constant_dynamic-update-slice_fusion.1
  291.4 1.1 convolution_subtract_fusion.1
  292.5 11.7 %cholesky.105 = f32[128,128]{1,0:T(8,128)S(1)} custom-call(f32[128,128]{1,0:T(8,128)S(1)} %convolution_subtract_fusion.1), custom_call_target="Cholesky" | custom-call | tf_op jit(solution)/shard_map/jit(cholesky)/cholesky | solution.py:29
  304.2 0.0 copy-start.2
  304.2 0.7 compare_reduce_fusion
  306.1 0.0 copy-done.2
  306.1 1.7 fusion.3
  307.8 0.1 triangular_solve.42
  307.9 5.0 %while.1 = (s32[]{:T(128)}, f32[256,256]{1,0:T(8,128)S(1)}, s32[2,2]{1,0:T(2,128)S(1)}, f32[2,128,128]{2,1,0:T(8,128)}, s32[]{:T(128)}) while((s32[]{:T(128)}, f32[256,256]{1,0:T(8,128)S(1)}, s32[2,2]{1,0:T(2,128)S(1)}, f32[2,128,128]{2,1,0:T(8,128)}, s32[]{:T(128)}) %tuple.29), condition=%wide.while_cond, body=%wide.while_body.sunk | while | flops 2 | bytes 132205 | solution.py:30
  307.9 0.6 fusion.23
  308.5 1.9 bitcast_dynamic-update-slice_fusion.2
  310.4 0.6 fusion.23
  311.0 1.9 bitcast_dynamic-update-slice_fusion.2
  312.9 20.5 %custom-call.15 = f32[2,128,128]{1,2,0:T(8,128)S(1)} custom-call(f32[2,128,128]{2,1,0:T(8,128)} %get-tuple-element.10), custom_call_target="InvertDiagBlocksLowerTriangular" | custom-call | tf_op jit(solution)/shard_map/triangular_solve | solution.py:30
  333.4 0.6 fusion.11
  334.0 0.6 convolution_subtract_fusion
  334.6 0.6 convolution_convert_fusion
  335.2 0.8 pad_maximum_fusion
  (8 shorter events, 0.1 us)
Async XLA Ops:
  7.2 1.6 copy-start
  7.2 78.5 %all-reduce.4.cloned.1.call-start = ((), (), s32[]{:S(2)}) async-start(), calls=%async_computation.1 | async-start | bytes 524288 | tf_op jit(solution)/shard_map/psum | solution.py:20
  11.8 121.4 %reduce-scatter.2.cloned.1.call-start = ((), (), s32[]{:S(2)}) async-start(), calls=%async_computation.2 | async-start | bytes 5242880 | tf_op jit(solution)/shard_map/reduce_scatter | solution.py:25
  86.7 2.7 copy-start.1
  89.4 176.5 %all-reduce.6.cloned.1.call-start = ((), (), s32[]{:S(2)}) async-start(), calls=%async_computation.3 | async-start | bytes 524288 | tf_op jit(solution)/shard_map/psum | solution.py:28
  268.0 0.7 copy-start.3
  304.2 1.9 copy-start.2
Sparse Core Ops, SparseCore 0:
  12.0 73.7 all-reduce.3
  89.5 43.6 reduce-scatter.1
  139.3 126.5 all-reduce.5
where the time goes:
time: 343 us
  waiting for transfers between devices  247 us (72%)
  other arithmetic  60.5 us (18%)
  between operations  15.1 us (4%)
  matrix products  11.5 us (3%)
  local copies, waits for them, and re-layouts  8.42 us (2%)
    psum x1, waiting for transfers between devices, shards(): gram = lax.psum(partial_gram, ('rows', 'cols'))  129 us
    psum x1, waiting for transfers between devices, shards(): coefficients = lax.psum(partial_value, 'rows') * coeff_scale  73.8 us
    reduce_scatter x1, waiting for transfers between devices, shards(): lax.psum_scatter(recon_part, 'cols', scatter_dimension=1, tiled=True)  43.7 us
    another operation x6, other arithmetic, shards(): factor = jnp.linalg.cholesky(gram)  34 us
    another operation x4, other arithmetic, shards(): lax.linalg.triangular_solve(factor, residual, left_side=True, lower=True)  23 us
  transfers between devices with their start and end apart: 3, of which 3 were waited for; matrix products, arithmetic and copies ran while one was open for 0% of the time, Pallas kernels for 0%

commit v1 on v0

--- a/solution.py
+++ b/solution.py
@@ -17,7 +17,7 @@
     partial_value = lax.dot_general(
         basis_cols, snapshots, (((0,), (1,)), ((), ())), preferred_element_type=jnp.float32
     )
-    coefficients = lax.psum(partial_value, "rows") * coeff_scale
+    coefficients = jnp.sum(lax.all_gather(partial_value, "rows"), axis=0) * coeff_scale
     coeff_low = coefficients.astype(jnp.bfloat16)
     recon_part = lax.dot_general(
         coeff_low, basis_cols, (((0,), (1,)), ((), ())), preferred_element_type=jnp.float32

time: 343 us -> 321 us (0.936)
  waiting for transfers between devices: 247 us -> 224 us
    psum x1 -> x0, waiting for transfers between devices: 73.8 us -> none  [shards(): coefficients = lax.psum(partial_value, 'rows') * coeff_scale]
    all_gather x0 -> x1, waiting for transfers between devices: none -> 51.9 us  [shards(): lax.all_gather(partial_value, 'rows')]
where the time goes in v1:
time: 321 us
  waiting for transfers between devices  224 us (70%)
  other arithmetic  61.3 us (19%)
  between operations  15.1 us (5%)
  matrix products  11.5 us (4%)
  local copies, waits for them, and re-layouts  8.42 us (3%)
    psum x1, waiting for transfers between devices, shards(): gram = lax.psum(partial_gram, ('rows', 'cols'))  129 us
    all_gather x1, waiting for transfers between devices, shards(): lax.all_gather(partial_value, 'rows')  51.9 us
    reduce_scatter x1, waiting for transfers between devices, shards(): lax.psum_scatter(recon_part, 'cols', scatter_dimension=1, tiled=True)  43.1 us
    another operation x6, other arithmetic, shards(): factor = jnp.linalg.cholesky(gram)  34 us
    another operation x4, other arithmetic, shards(): lax.linalg.triangular_solve(factor, residual, left_side=True, lower=True)  23 us
  transfers between devices with their start and end apart: 3, of which 3 were waited for; matrix products, arithmetic and copies ran while one was open for 0% of the time, Pallas kernels for 0%

profile of v1, /device:TPU:0, one launch (start us, length us, event | category | flops | bytes accessed | tf_op | source)
XLA Modules:
  0.0 320.8 jit_solution(12967670436428104753)
XLA Ops:
  7.2 0.0 copy-start
  7.2 0.0 all-gather.3.cloned.1.call-start
  7.2 1.5 copy-done
  8.8 3.0 fusion.12
  11.8 0.0 all-gather.3.cloned.1.call-update
  11.8 0.0 reduce-scatter.2.cloned.1.call-start
  11.9 51.9 %all-gather.3.cloned.1.call-done = f32[2048,256]{1,0:T(8,128)} async-done(((f32[256,256]{1,0:T(8,128)}), f32[2048,256]{1,0:T(8,128)}) %all-gather.3.cloned.1.call-update) | async-done | bytes 2097168 | tf_op jit(solution)/shard_map/all_gather | solution.py:20
  63.8 1.8 reduce_sum.9
  65.6 0.0 copy-start.1
  65.6 2.7 fusion.4
  68.3 0.0 copy-done.1
  68.3 0.0 reduce-scatter.2.cloned.1.call-update
  68.3 0.0 all-reduce.3.cloned.1.call-start
  68.4 43.1 %reduce-scatter.2.cloned.1.call-done = f32[256,1024]{1,0:T(8,128)} async-done(((f32[256,4096]{1,0:T(8,128)}), f32[256,1024]{1,0:T(8,128)}) %reduce-scatter.2.cloned.1.call-update) | async-done | bytes 1048592 | tf_op jit(solution)/shard_map/reduce_scatter | solution.py:25
  111.5 1.5 multiply_subtract_fusion
  113.0 1.7 convolution_multiply_fusion
  114.7 0.0 all-reduce.3.cloned.1.call-update
  114.8 129.3 %all-reduce.3.cloned.1.call-done = f32[256,256]{0,1:T(8,128)} async-done(((f32[256,256]{0,1:T(8,128)}), f32[256,256]{0,1:T(8,128)}) %all-reduce.3.cloned.1.call-update) | async-done | bytes 262160 | tf_op jit(solution)/shard_map/psum | solution.py:28
  244.1 1.1 copy.6
  245.2 1.0 fusion.2
  246.2 0.0 copy-start.3
  246.2 0.7 copy-done.3
  246.9 11.7 %cholesky.50 = f32[128,128]{1,0:T(8,128)S(1)} custom-call(f32[128,128]{1,0:T(8,128)S(1)} %cholesky.118), custom_call_target="Cholesky" | custom-call | tf_op jit(solution)/shard_map/jit(cholesky)/cholesky | solution.py:29
  258.7 9.8 %custom-call.14 = f32[1,128,128]{1,2,0:T(8,128)S(1)} custom-call(f32[1,128,128]{2,1,0:T(8,128)S(1)} %get-tuple-element.26), custom_call_target="InvertDiagBlocksLowerTriangular" | custom-call | tf_op jit(solution)/shard_map/jit(cholesky)/cholesky | solution.py:29
  268.5 1.0 constant_dynamic-update-slice_fusion.1
  269.5 1.1 convolution_subtract_fusion.1
  270.6 11.7 %cholesky.105 = f32[128,128]{1,0:T(8,128)S(1)} custom-call(f32[128,128]{1,0:T(8,128)S(1)} %convolution_subtract_fusion.1), custom_call_target="Cholesky" | custom-call | tf_op jit(solution)/shard_map/jit(cholesky)/cholesky | solution.py:29
  282.4 0.0 copy-start.2
  282.4 0.7 compare_reduce_fusion
  284.3 0.0 copy-done.2
  284.3 1.7 fusion.3
  286.0 0.1 triangular_solve.42
  286.0 5.0 %while.1 = (s32[]{:T(128)}, f32[256,256]{1,0:T(8,128)S(1)}, s32[2,2]{1,0:T(2,128)S(1)}, f32[2,128,128]{2,1,0:T(8,128)}, s32[]{:T(128)}) while((s32[]{:T(128)}, f32[256,256]{1,0:T(8,128)S(1)}, s32[2,2]{1,0:T(2,128)S(1)}, f32[2,128,128]{2,1,0:T(8,128)}, s32[]{:T(128)}) %tuple.29), condition=%wide.while_cond, body=%wide.while_body.sunk | while | flops 2 | bytes 132205 | solution.py:30
  286.0 0.6 fusion.23
  286.6 1.9 bitcast_dynamic-update-slice_fusion.2
  288.6 0.6 fusion.23
  289.1 1.9 bitcast_dynamic-update-slice_fusion.2
  291.0 20.5 %custom-call.15 = f32[2,128,128]{1,2,0:T(8,128)S(1)} custom-call(f32[2,128,128]{2,1,0:T(8,128)} %get-tuple-element.10), custom_call_target="InvertDiagBlocksLowerTriangular" | custom-call | tf_op jit(solution)/shard_map/triangular_solve | solution.py:30
  311.5 0.6 fusion.11
  312.2 0.6 convolution_subtract_fusion
  312.8 0.6 convolution_convert_fusion
  313.4 0.8 pad_maximum_fusion
  (9 shorter events, 0.1 us)
Async XLA Ops:
  7.2 1.6 copy-start
  7.2 56.6 %all-gather.3.cloned.1.call-start = ((), (), s32[]{:S(2)}) async-start(), calls=%async_computation.3 | async-start | bytes 2359296 | tf_op jit(solution)/shard_map/all_gather | solution.py:20
  11.8 99.6 %reduce-scatter.2.cloned.1.call-start = ((), (), s32[]{:S(2)}) async-start(), calls=%async_computation.1 | async-start | bytes 5242880 | tf_op jit(solution)/shard_map/reduce_scatter | solution.py:25
  65.6 2.7 copy-start.1
  68.3 175.8 %all-reduce.3.cloned.1.call-start = ((), (), s32[]{:S(2)}) async-start(), calls=%async_computation.2 | async-start | bytes 524288 | tf_op jit(solution)/shard_map/psum | solution.py:28
  246.2 0.7 copy-start.3
  282.4 1.9 copy-start.2
Sparse Core Ops, SparseCore 0:
  12.0 51.7 all-gather.2
  68.5 42.9 reduce-scatter.1
  117.5 126.5 all-reduce.2

commit v2 on v0

--- a/solution.py
+++ b/solution.py
@@ -25,7 +25,7 @@
     recon = lax.psum_scatter(recon_part, "cols", scatter_dimension=1, tiled=True) / math.sqrt(RANK)
     residual = own_snaps.astype(jnp.float32) - recon
     partial_gram = jnp.dot(residual, residual.T, precision=lax.Precision.HIGHEST) / total_points
-    gram = lax.psum(partial_gram, ("rows", "cols"))
+    gram = lax.psum(lax.psum(partial_gram, "rows"), "cols")
     factor = jnp.linalg.cholesky(gram)
     directions = lax.linalg.triangular_solve(factor, residual, left_side=True, lower=True).astype(
         jnp.bfloat16

time: 343 us -> 319 us (0.930)
  waiting for transfers between devices: 247 us -> 223 us
    psum x1 -> x2, waiting for transfers between devices: 129 us -> 105 us  [shards(): gram = lax.psum(lax.psum(partial_gram, 'rows'), 'cols')]
  transfers between devices with their start and end apart: 3 -> 4, of which waited for: 3 -> 4; matrix products, arithmetic and copies ran while one was open for 0% -> 0% of each run, Pallas kernels for 0% -> 0%
where the time goes in v2:
time: 319 us
  waiting for transfers between devices  223 us (70%)
  other arithmetic  60.5 us (19%)
  between operations  15.1 us (5%)
  matrix products  11.5 us (4%)
  local copies, waits for them, and re-layouts  8.42 us (3%)
    psum x2, waiting for transfers between devices, shards(): gram = lax.psum(lax.psum(partial_gram, 'rows'), 'cols')  105 us
    psum x1, waiting for transfers between devices, shards(): coefficients = lax.psum(partial_value, 'rows') * coeff_scale  73.8 us
    reduce_scatter x1, waiting for transfers between devices, shards(): lax.psum_scatter(recon_part, 'cols', scatter_dimension=1, tiled=True)  43.7 us
    another operation x6, other arithmetic, shards(): factor = jnp.linalg.cholesky(gram)  34 us
    another operation x4, other arithmetic, shards(): lax.linalg.triangular_solve(factor, residual, left_side=True, lower=True)  23 us
  transfers between devices with their start and end apart: 4, of which 4 were waited for; matrix products, arithmetic and copies ran while one was open for 0% of the time, Pallas kernels for 0%

profile of v2, /device:TPU:0, one launch (start us, length us, event | category | flops | bytes accessed | tf_op | source)
XLA Modules:
  0.0 318.6 jit_solution(7522622275943679476)
XLA Ops:
  7.2 0.0 copy-start
  7.2 0.0 all-reduce.5.cloned.1.call-start
  7.2 1.5 copy-done
  8.8 3.0 fusion.12
  11.8 0.0 all-reduce.5.cloned.1.call-update
  11.8 0.0 reduce-scatter.2.cloned.1.call-start
  11.9 73.8 %all-reduce.5.cloned.1.call-done = f32[256,256]{1,0:T(8,128)} async-done(((f32[256,256]{1,0:T(8,128)}), f32[256,256]{1,0:T(8,128)}) %all-reduce.5.cloned.1.call-update) | async-done | bytes 262160 | tf_op jit(solution)/shard_map/psum | solution.py:20
  85.7 1.0 broadcast_multiply_fusion
  86.7 0.0 copy-start.1
  86.7 2.7 fusion.4
  89.4 0.0 copy-done.1
  89.4 0.0 reduce-scatter.2.cloned.1.call-update
  89.4 0.0 all-reduce.7.cloned.1.call-start
  89.5 43.7 %reduce-scatter.2.cloned.1.call-done = f32[256,1024]{1,0:T(8,128)} async-done(((f32[256,4096]{1,0:T(8,128)}), f32[256,1024]{1,0:T(8,128)}) %reduce-scatter.2.cloned.1.call-update) | async-done | bytes 1048592 | tf_op jit(solution)/shard_map/reduce_scatter | solution.py:25
  133.2 1.5 multiply_subtract_fusion
  134.8 1.7 convolution_multiply_fusion
  136.5 0.0 all-reduce.7.cloned.1.call-update
  136.5 0.2 all-reduce.9.cloned.1.call-start
  136.8 71.5 %all-reduce.7.cloned.1.call-done = f32[256,256]{0,1:T(8,128)} async-done(((f32[256,256]{0,1:T(8,128)}), f32[256,256]{0,1:T(8,128)}) %all-reduce.7.cloned.1.call-update) | async-done | bytes 262160 | tf_op jit(solution)/shard_map/psum | solution.py:28
  208.2 0.0 all-reduce.9.cloned.1.call-update
  208.3 33.7 %all-reduce.9.cloned.1.call-done = f32[256,256]{0,1:T(8,128)} async-done(((f32[256,256]{0,1:T(8,128)}), f32[256,256]{0,1:T(8,128)}) %all-reduce.9.cloned.1.call-update) | async-done | bytes 262160 | tf_op jit(solution)/shard_map/psum | solution.py:28
  241.9 1.1 copy.6
  243.0 1.0 fusion.2
  244.0 0.0 copy-start.3
  244.0 0.7 copy-done.3
  244.7 11.7 %cholesky.50 = f32[128,128]{1,0:T(8,128)S(1)} custom-call(f32[128,128]{1,0:T(8,128)S(1)} %cholesky.118), custom_call_target="Cholesky" | custom-call | tf_op jit(solution)/shard_map/jit(cholesky)/cholesky | solution.py:29
  256.5 9.8 %custom-call.14 = f32[1,128,128]{1,2,0:T(8,128)S(1)} custom-call(f32[1,128,128]{2,1,0:T(8,128)S(1)} %get-tuple-element.26), custom_call_target="InvertDiagBlocksLowerTriangular" | custom-call | tf_op jit(solution)/shard_map/jit(cholesky)/cholesky | solution.py:29
  266.3 1.0 constant_dynamic-update-slice_fusion.1
  267.4 1.1 convolution_subtract_fusion.1
  268.5 11.7 %cholesky.105 = f32[128,128]{1,0:T(8,128)S(1)} custom-call(f32[128,128]{1,0:T(8,128)S(1)} %convolution_subtract_fusion.1), custom_call_target="Cholesky" | custom-call | tf_op jit(solution)/shard_map/jit(cholesky)/cholesky | solution.py:29
  280.2 0.0 copy-start.2
  280.2 0.7 compare_reduce_fusion
  282.1 0.0 copy-done.2
  282.1 1.7 fusion.3
  283.8 0.1 triangular_solve.42
  283.9 5.0 %while.1 = (s32[]{:T(128)}, f32[256,256]{1,0:T(8,128)S(1)}, s32[2,2]{1,0:T(2,128)S(1)}, f32[2,128,128]{2,1,0:T(8,128)}, s32[]{:T(128)}) while((s32[]{:T(128)}, f32[256,256]{1,0:T(8,128)S(1)}, s32[2,2]{1,0:T(2,128)S(1)}, f32[2,128,128]{2,1,0:T(8,128)}, s32[]{:T(128)}) %tuple.29), condition=%wide.while_cond, body=%wide.while_body.sunk | while | flops 2 | bytes 132205 | solution.py:30
  283.9 0.6 fusion.23
  284.5 1.9 bitcast_dynamic-update-slice_fusion.2
  286.4 0.6 fusion.23
  287.0 1.9 bitcast_dynamic-update-slice_fusion.2
  288.9 20.5 %custom-call.15 = f32[2,128,128]{1,2,0:T(8,128)S(1)} custom-call(f32[2,128,128]{2,1,0:T(8,128)} %get-tuple-element.10), custom_call_target="InvertDiagBlocksLowerTriangular" | custom-call | tf_op jit(solution)/shard_map/triangular_solve | solution.py:30
  309.4 0.6 fusion.11
  310.0 0.6 convolution_subtract_fusion
  310.6 0.6 convolution_convert_fusion
  311.3 0.8 pad_maximum_fusion
  (8 shorter events, 0.1 us)
Async XLA Ops:
  7.2 1.6 copy-start
  7.2 78.5 %all-reduce.5.cloned.1.call-start = ((), (), s32[]{:S(2)}) async-start(), calls=%async_computation.1 | async-start | bytes 524288 | tf_op jit(solution)/shard_map/psum | solution.py:20
  11.8 121.4 %reduce-scatter.2.cloned.1.call-start = ((), (), s32[]{:S(2)}) async-start(), calls=%async_computation.2 | async-start | bytes 5242880 | tf_op jit(solution)/shard_map/reduce_scatter | solution.py:25
  86.7 2.7 copy-start.1
  89.4 118.8 %all-reduce.7.cloned.1.call-start = ((), (), s32[]{:S(2)}) async-start(), calls=%async_computation.3 | async-start | bytes 524288 | tf_op jit(solution)/shard_map/psum | solution.py:28
  136.5 105.4 %all-reduce.9.cloned.1.call-start = ((), (), s32[]{:S(2)}) async-start(), calls=%async_computation.4 | async-start | bytes 524288 | tf_op jit(solution)/shard_map/psum | solution.py:28
  244.0 0.7 copy-start.3
  280.2 1.9 copy-start.2
Sparse Core Ops, SparseCore 0:
  12.0 73.7 all-reduce.4
  89.5 43.6 reduce-scatter.1
  137.2 71.0 all-reduce.6
  210.4 31.4 all-reduce.8
